TPU v7x, 32 devices: a whole 2x2x4 slice. The times are simulated.
32 devices in a mesh: space: 8 (over z, y), chan: 2 (over core), filt: 2 (over x).
Axes of the slice: x: 2, y: 2, z: 4, core: 2. Of those that a mesh axis runs over, the one named last changes fastest.
Arguments:
- activation: bfloat16 [8, 512, 512], P('space', ('chan', 'filt')), may hold values from -6 to 6
- kernel: bfloat16 [3, 3, 3, 512, 512], P(None, None, None, 'filt', 'chan'), may hold values from -0.0546875 to 0.0546875
- out_grad: bfloat16 [8, 512, 512], P('space', 'filt', 'chan'), may hold values from -6 to 6
Outputs:
- output: bfloat16 [8, 512, 512], P('space', 'filt', 'chan')
- input_grad: bfloat16 [8, 512, 512], P('space', ('chan', 'filt'))
- kernel_grad: float32 [3, 3, 3, 512, 512], P(None, None, None, 'filt', 'chan')
All inputs are finite; a program needn't handle non-finite values.
Results may differ from a plain program's by a relative error of at most 0.001.
Values may be sent and summed in bfloat16 or wider, within the bound.
A program may use at most 128 MiB of HBM per device.

v0:
```python
import jax
import jax.numpy as jnp
from jax import lax
from jax.sharding import PartitionSpec as P

W = 16


def padded(x, sides, width):
    for axis, dim in sides:
        size, length = (lax.axis_size(axis), x.shape[dim])
        up = [(i, (i + 1) % size) for i in range(size - 1)]
        down = [(j, i) for i, j in up]
        last = lax.slice_in_dim(x, length - width, length, axis=dim)
        first = lax.slice_in_dim(x, 0, width, axis=dim)
        before = lax.ppermute(last, axis, up)
        after = lax.ppermute(first, axis, down)
        x = jnp.concatenate([before, x, after], axis=dim)
    return x


def plane_window(widened, plane, row_step, col_step, masks):
    begin = row_step * W + col_step
    return widened[:, :, begin : begin + plane] * masks[col_step]


def body(activation, kernel, out_grad):
    depth = activation.shape[0]
    plane = activation.shape[2]
    panels = lax.all_gather(activation, "filt", axis=1, tiled=True)
    rimmed = padded(panels, (("space", 0),), 1)
    grad_full = lax.all_gather(out_grad, "chan", axis=2, tiled=True)
    grad_rimmed = padded(grad_full, (("space", 0),), 1)
    column = lax.iota(jnp.int32, plane) % W
    masks = [
        ((column + step - 1 >= 0) & (column + step - 1 < W)).astype(jnp.bfloat16)
        for step in range(3)
    ]
    chan_local = rimmed.shape[1]
    filt_local = grad_rimmed.shape[1]
    wide_input = jnp.pad(rimmed, ((0, 0), (0, 0), (W + 1, W + 1)))
    wide_grad = jnp.pad(grad_rimmed, ((0, 0), (0, 0), (W + 1, W + 1)))
    forward = jnp.zeros((depth, filt_local, plane), jnp.float32)
    backward = jnp.zeros((depth, chan_local, plane), jnp.float32)
    taps = []
    for a in range(3):
        input_slab = wide_input[a : a + depth]
        grad_slab = wide_grad[2 - a : 2 - a + depth]
        for b in range(3):
            window = jnp.concatenate(
                [plane_window(input_slab, plane, b, c, masks) for c in range(3)], axis=1
            )
            grad_window = jnp.concatenate(
                [plane_window(grad_slab, plane, 2 - b, 2 - c, masks) for c in range(3)], axis=1
            )
            weights = kernel[a, b]
            forward_weights = weights.transpose(1, 0, 2).reshape(filt_local, 3 * chan_local)
            backward_weights = weights.reshape(3 * filt_local, chan_local)
            forward = forward + jnp.einsum(
                "fk,zkp->zfp", forward_weights, window, preferred_element_type=jnp.float32
            )
            backward = backward + jnp.einsum(
                "fk,zfp->zkp", backward_weights, grad_window, preferred_element_type=jnp.float32
            )
            joined = jnp.einsum(
                "zfp,zkp->fk", grad_full, window, preferred_element_type=jnp.float32
            )
            taps.append(joined.reshape(filt_local, 3, chan_local).transpose(1, 0, 2))
    output = lax.psum_scatter(forward, "chan", scatter_dimension=2, tiled=True).astype(jnp.bfloat16)
    input_grad = lax.psum_scatter(backward, "filt", scatter_dimension=1, tiled=True).astype(
        jnp.bfloat16
    )
    local_grad = jnp.stack(taps).reshape(3, 3, 3, filt_local, chan_local)
    total = lax.psum(local_grad, "space")
    cells = depth * lax.axis_size("space") * plane
    kernel_grad = total / jnp.sqrt(jnp.float32(cells))
    return (output, input_grad, kernel_grad)


def solution(mesh):
    placed = (
        P("space", ("chan", "filt"), None),
        P(None, None, None, "filt", "chan"),
        P("space", "filt", "chan"),
    )
    return jax.shard_map(
        body,
        mesh=mesh,
        in_specs=placed,
        out_specs=(
            P("space", "filt", "chan"),
            P("space", ("chan", "filt"), None),
            P(None, None, None, "filt", "chan"),
        ),
        check_vma=False,
    )
```

profile of v0, /device:TPU:0, one launch (start us, length us, event | category | flops | bytes accessed | tf_op | source)
XLA Modules:
  0.0 349.9 jit_solution(17022431209506651574)
XLA Ops:
  8.0 7.4 %all_gather.6 = bf16[1,256,512]{2,1,0:T(8,128)(2,1)S(1)} all-gather(bf16[1,128,512]{2,1,0:T(8,128)(2,1)} %param.3), channel_id=1, replica_groups=mesh['space'=8,'chan'=2,'filt'=2] {'filt'}, dimensions={1}, use_global_device_ids=true | all-gather | bytes 393216 | tf_op jit(solution)/shard_map/all_gather | solution.py:30
  15.4 1.3 collective-permute-start.1
  16.7 5.3 %collective-permute-start = (bf16[1,256,512]{2,1,0:T(8,128)(2,1)S(1)}, bf16[1,256,512]{2,1,0:T(8,128)(2,1)}, u32[]{:S(2)}, u32[]{:S(2)}) collective-permute-start(bf16[1,256,512]{2,1,0:T(8,128)(2,1)S(1)} %all_gather.6), channel_id=1, source_target_pairs={{0,4},{4,8},{8,12},{12,16},{16,20},{20,24},{24,28},{1,5},{5,9},{9,... | collective-permute-start | bytes 786440 | tf_op jit(solution)/shard_map/ppermute | solution.py:16
  22.0 2.3 all_gather.7
  24.2 4.5 %collective-permute-start.2 = (bf16[1,256,512]{2,1,0:T(8,128)(2,1)S(1)}, bf16[1,256,512]{2,1,0:T(8,128)(2,1)}, u32[]{:S(2)}, u32[]{:S(2)}) collective-permute-start(bf16[1,256,512]{2,1,0:T(8,128)(2,1)S(1)} %all_gather.7), channel_id=1, source_target_pairs={{0,4},{4,8},{8,12},{12,16},{16,20},{20,24},{24,28},{1,5},{5,9},{9,... | collective-permute-start | bytes 786440 | tf_op jit(solution)/shard_map/ppermute | solution.py:16
  28.8 1.3 collective-permute-start.3
  30.1 3.2 fusion.87
  33.3 2.3 copy.42
  35.6 1.9 copy.43
  37.5 0.9 copy.44
  38.5 0.9 copy.45
  39.4 0.9 copy.46
  40.3 0.9 copy.47
  41.2 0.9 copy.48
  42.2 1.0 copy.49
  43.1 0.9 copy.50
  44.1 1.5 select_maximum_fusion.2
  45.6 0.7 slice_multiply_fusion.24
  46.3 1.6 select_maximum_fusion
  48.0 1.9 slice_multiply_fusion
  49.8 2.8 slice_multiply_fusion.26
  53.0 4.0 %slice_multiply_fusion.2 = (bf16[1,256,512]{2,1,0:T(8,128)(2,1)}, bf16[1,256,512]{2,1,0:T(8,128)(2,1)}, bf16[1,256,512]{2,1,0:T(8,128)(2,1)}, bf16[1,256,512]{2,...) fusion(bf16[3,256,546]{2,1,0:T(8,128)(2,1)S(1)} %select_maximum, ...), kind=kLoop, calls=%fused_computation.112 | loop fusion | flops 2228224 | bytes 8914944 | tf_op jit(solution)/shard_map/mul | solution.py:24
  57.1 0.9 copy-done.34
  58.4 0.6 copy-done.33
  59.4 1.1 pad_maximum_fusion.2
  61.9 1.2 pad_maximum_fusion.4
  64.6 1.8 broadcast_multiply_fusion.3
  66.4 1.3 pad_maximum_fusion.6
  68.6 1.2 fusion.10
  70.1 1.6 fusion.13
  77.9 0.9 copy-done.10
  81.5 1.2 fusion.11
  82.8 1.3 fusion.9
  84.1 1.3 fusion.8
  85.4 1.3 fusion.7
  86.7 1.3 fusion.6
  88.0 1.3 fusion.5
  89.3 1.3 fusion.4
  90.5 1.3 fusion.3
  91.8 1.3 fusion.2
  93.1 1.3 fusion.1
  94.4 8.1 %copy.39 = f32[3,3,3,256,256]{4,3,2,1,0:T(8,128)} copy(f32[3,3,3,256,256]{3,4,2,1,0:T(8,128)} %bitcast.227) | data formatting | bytes 14155776 | tf_op jit(solution)/shard_map/reshape | solution.py:73
  102.5 1.0 convert_element_type.135
  103.5 0.8 copy.40
  104.3 1.0 convert_element_type.136
  105.2 0.8 copy.41
  106.0 229.8 %all-reduce.4.cloned.1.call-done = f32[3,3,3,256,256]{4,3,2,1,0:T(8,128)} async-done(((f32[3,3,3,256,256]{4,3,2,1,0:T(8,128)}), f32[3,3,3,256,256]{4,3,2,1,0:T(8,128)}) %all-reduce.4.cloned.1.call-update) | async-done | bytes 7077904 | tf_op jit(solution)/shard_map/psum | solution.py:74
  335.8 6.7 %broadcast_multiply_fusion = f32[3,3,3,256,256]{4,3,2,1,0:T(8,128)} fusion(f32[3,3,3,256,256]{4,3,2,1,0:T(8,128)} %all-reduce.4.cloned.1.call-done), kind=kLoop, calls=%fused_computation | loop fusion | flops 1769472 | bytes 14155776 | tf_op jit(solution)/shard_map/div | solution.py:76
  (149 shorter events, 14.3 us)
Async XLA Ops:
  8.0 94.5 %reduce-scatter.3.cloned.1.call-start = ((), (), s32[]{:S(2)}) async-start(), calls=%async_computation.2 | async-start | bytes 786432 | tf_op jit(solution)/shard_map/reduce_scatter | solution.py:69
  15.4 28.7 %collective-permute-start.1 = (bf16[1,256,512]{2,1,0:T(8,128)(2,1)S(1)}, bf16[1,256,512]{2,1,0:T(8,128)(2,1)}, u32[]{:S(2)}, u32[]{:S(2)}) collective-permute-start(bf16[1,256,512]{2,1,0:T(8,128)(2,1)S(1)} %all_gather.6), channel_id=1, source_target_pairs={{4,0},{8,4},{12,8},{16,12},{20,16},{24,20},{28,24},{5,1},{9,5},{13... | collective-permute-start | bytes 786440 | tf_op jit(solution)/shard_map/ppermute | solution.py:17
  16.7 27.4 %collective-permute-start = (bf16[1,256,512]{2,1,0:T(8,128)(2,1)S(1)}, bf16[1,256,512]{2,1,0:T(8,128)(2,1)}, u32[]{:S(2)}, u32[]{:S(2)}) collective-permute-start(bf16[1,256,512]{2,1,0:T(8,128)(2,1)S(1)} %all_gather.6), channel_id=1, source_target_pairs={{0,4},{4,8},{8,12},{12,16},{16,20},{20,24},{24,28},{1,5},{5,9},{9,... | collective-permute-start | bytes 786440 | tf_op jit(solution)/shard_map/ppermute | solution.py:16
  24.2 22.1 %collective-permute-start.2 = (bf16[1,256,512]{2,1,0:T(8,128)(2,1)S(1)}, bf16[1,256,512]{2,1,0:T(8,128)(2,1)}, u32[]{:S(2)}, u32[]{:S(2)}) collective-permute-start(bf16[1,256,512]{2,1,0:T(8,128)(2,1)S(1)} %all_gather.7), channel_id=1, source_target_pairs={{0,4},{4,8},{8,12},{12,16},{16,20},{20,24},{24,28},{1,5},{5,9},{9,... | collective-permute-start | bytes 786440 | tf_op jit(solution)/shard_map/ppermute | solution.py:16
  28.8 17.6 %collective-permute-start.3 = (bf16[1,256,512]{2,1,0:T(8,128)(2,1)S(1)}, bf16[1,256,512]{2,1,0:T(8,128)(2,1)}, u32[]{:S(2)}, u32[]{:S(2)}) collective-permute-start(bf16[1,256,512]{2,1,0:T(8,128)(2,1)S(1)} %all_gather.7), channel_id=1, source_target_pairs={{4,0},{8,4},{12,8},{16,12},{20,16},{24,20},{28,24},{5,1},{9,5},{13... | collective-permute-start | bytes 786440 | tf_op jit(solution)/shard_map/ppermute | solution.py:17
  33.3 6.1 %copy-start.15 = (bf16[1,1,3,256,256]{4,3,2,1,0:T(8,128)(2,1)}, bf16[1,1,3,256,256]{4,3,2,1,0:T(8,128)(2,1)S(1)}, u32[]{:S(2)}) copy-start(bf16[1,1,3,256,256]{4,3,2,1,0:T(8,128)(2,1)S(1)} %get-tuple-element.17) | copy-start | bytes 1179652
  33.3 6.1 %copy-start.17 = (bf16[1,1,3,256,256]{4,3,2,1,0:T(8,128)(2,1)}, bf16[1,1,3,256,256]{4,3,2,1,0:T(8,128)(2,1)S(1)}, u32[]{:S(2)}) copy-start(bf16[1,1,3,256,256]{4,3,2,1,0:T(8,128)(2,1)S(1)} %get-tuple-element.18) | copy-start | bytes 1179652
  33.3 6.1 %copy-start.13 = (bf16[1,1,3,256,256]{4,3,2,1,0:T(8,128)(2,1)}, bf16[1,1,3,256,256]{4,3,2,1,0:T(8,128)(2,1)S(1)}, u32[]{:S(2)}) copy-start(bf16[1,1,3,256,256]{4,3,2,1,0:T(8,128)(2,1)S(1)} %get-tuple-element.16) | copy-start | bytes 1179652
  33.3 7.0 %copy-start.11 = (bf16[1,1,3,256,256]{4,3,2,1,0:T(8,128)(2,1)}, bf16[1,1,3,256,256]{4,3,2,1,0:T(8,128)(2,1)S(1)}, u32[]{:S(2)}) copy-start(bf16[1,1,3,256,256]{4,3,2,1,0:T(8,128)(2,1)S(1)} %get-tuple-element.15) | copy-start | bytes 1179652
  33.3 7.9 %copy-start.9 = (bf16[1,1,3,256,256]{4,3,2,1,0:T(8,128)(2,1)}, bf16[1,1,3,256,256]{4,3,2,1,0:T(8,128)(2,1)S(1)}, u32[]{:S(2)}) copy-start(bf16[1,1,3,256,256]{4,3,2,1,0:T(8,128)(2,1)S(1)} %get-tuple-element.14) | copy-start | bytes 1179652
  33.3 8.8 %copy-start.7 = (bf16[1,1,3,256,256]{4,3,2,1,0:T(8,128)(2,1)}, bf16[1,1,3,256,256]{4,3,2,1,0:T(8,128)(2,1)S(1)}, u32[]{:S(2)}) copy-start(bf16[1,1,3,256,256]{4,3,2,1,0:T(8,128)(2,1)S(1)} %get-tuple-element.13) | copy-start | bytes 1179652
  33.3 9.8 %copy-start.5 = (bf16[1,1,3,256,256]{4,3,2,1,0:T(8,128)(2,1)}, bf16[1,1,3,256,256]{4,3,2,1,0:T(8,128)(2,1)S(1)}, u32[]{:S(2)}) copy-start(bf16[1,1,3,256,256]{4,3,2,1,0:T(8,128)(2,1)S(1)} %get-tuple-element.12) | copy-start | bytes 1179652
  46.3 21.7 %copy-start.21 = (bf16[1,256,512]{2,1,0:T(8,128)(2,1)}, bf16[1,256,512]{2,1,0:T(8,128)(2,1)S(1)}, u32[]{:S(2)}) copy-start(bf16[1,256,512]{2,1,0:T(8,128)(2,1)S(1)} %get-tuple-element.60) | copy-start | bytes 786436
  49.8 2.8 copy-start.35
  52.6 15.5 %copy-start.23 = (bf16[1,256,512]{2,1,0:T(8,128)(2,1)}, bf16[1,256,512]{2,1,0:T(8,128)(2,1)S(1)}, u32[]{:S(2)}) copy-start(bf16[1,256,512]{2,1,0:T(8,128)(2,1)S(1)} %get-tuple-element.45) | copy-start | bytes 786436
  52.6 15.5 %copy-start.25 = (bf16[1,256,512]{2,1,0:T(8,128)(2,1)}, bf16[1,256,512]{2,1,0:T(8,128)(2,1)S(1)}, u32[]{:S(2)}) copy-start(bf16[1,256,512]{2,1,0:T(8,128)(2,1)S(1)} %get-tuple-element.80) | copy-start | bytes 786436
  61.9 1.3 copy-start.30
  66.4 1.3 copy-start.28
  68.6 1.5 copy-start.20
  69.9 34.4 %reduce-scatter.5.cloned.1.call-start = ((), (), s32[]{:S(2)}) async-start(), calls=%async_computation.3 | async-start | bytes 786432 | tf_op jit(solution)/shard_map/reduce_scatter | solution.py:70
  70.1 1.7 copy-start.19
  70.1 1.7 copy-start.46
  70.1 1.7 copy-start.58
  70.1 1.7 copy-start.59
  71.8 1.1 copy-start.56
  71.8 1.2 copy-start.57
  73.0 1.1 copy-start.54
  73.0 1.2 copy-start.55
  74.3 1.1 copy-start.41
  74.3 1.1 copy-start.47
  74.3 1.2 copy-start.53
  75.5 1.1 copy-start.51
  75.5 1.2 copy-start.52
  76.7 1.1 copy-start.26
  77.8 1.1 copy-start.38
  77.8 1.2 copy-start.49
  77.8 1.2 copy-start.50
  79.1 1.1 copy-start.37
  79.1 1.2 copy-start.40
  79.1 1.2 copy-start.48
  80.3 1.1 copy-start.44
  80.3 1.2 copy-start.45
  84.0 1.4 copy-start
  84.1 251.7 %all-reduce.4.cloned.1.call-start = ((), (), s32[]{:S(2)}) async-start(), calls=%async_computation.4 | async-start | bytes 14155776 | tf_op jit(solution)/shard_map/psum | solution.py:74
  85.4 2.6 copy-start.2
  86.7 2.6 copy-start.1
  88.0 2.6 copy-start.4
  89.3 2.6 copy-start.3
  (19 other events, 19.3 us)
Sparse Core Ops, SparseCore 0:
  70.0 9.3 reduce-scatter.2
  84.2 16.0 reduce-scatter.4
Sparse Core Ops, SparseCore 1:
  102.6 233.1 all-reduce.3
where the time goes:
time: 351 us; the launch traced here: 350 us
  waiting for transfers between devices  230 us (66%)
  local copies, waits for them, and re-layouts  33.5 us (10%)
  other arithmetic  26.6 us (8%)
  matrix products  21.7 us (6%)
  between operations  16 us (5%)
  starting transfers between devices  12.7 us (4%)
  blocking collectives  9.65 us (3%)
    psum x1, waiting for transfers between devices, body(): total = lax.psum(local_grad, 'space')  230 us
    unnamed x131, local copies, waits for them, and re-layouts  22.2 us
    dot_general x9, matrix products, body(): jnp.einsum('zfp,zkp->fk', grad_full, window, preferred_element_type=jnp.f...  11.5 us
    mul x5, other arithmetic, plane_window(): return widened[:, :, begin:begin + plane] * masks[col_step]  11.1 us
    ppermute x2, starting transfers between devices, padded(): before = lax.ppermute(last, axis, up)  9.8 us
    reshape x1, local copies, waits for them, and re-layouts, body(): local_grad = jnp.stack(taps).reshape(3, 3, 3, filt_local, chan_local)  8.09 us
    all_gather x1, blocking collectives, body(): panels = lax.all_gather(activation, 'filt', axis=1, tiled=True)  7.36 us
  transfers between devices with their start and end apart: 7, of which 1 were waited for; matrix products, arithmetic and copies ran while one was open for 13% of the time, Pallas kernels for 0%

commit v1 on v0

--- a/solution.py
+++ b/solution.py
@@ -71,7 +71,7 @@
         jnp.bfloat16
     )
     local_grad = jnp.stack(taps).reshape(3, 3, 3, filt_local, chan_local)
-    total = lax.psum(local_grad, "space")
+    total = jnp.sum(lax.all_gather(local_grad, "space"), axis=0)
     cells = depth * lax.axis_size("space") * plane
     kernel_grad = total / jnp.sqrt(jnp.float32(cells))
     return (output, input_grad, kernel_grad)

time: 351 us -> 1220 us (3.48)
  waiting for transfers between devices: 230 us -> 1070 us
  other arithmetic: 26.6 us -> 47.1 us
  local copies, waits for them, and re-layouts: 33.5 us -> 46.5 us
    all_gather x0 -> x1, waiting for transfers between devices: none -> 1070 us  [body(): total = jnp.sum(lax.all_gather(local_grad, 'space'), axis=0)]
    psum x1 -> x0, waiting for transfers between devices: 230 us -> none  [body(): total = lax.psum(local_grad, 'space')]
    reduce_sum x0 -> x1, other arithmetic: none -> 21.5 us  [body(): total = jnp.sum(lax.all_gather(local_grad, 'space'), axis=0)]
    unnamed x131 -> x105, local copies, waits for them, and re-layouts: 22.2 us -> 35.3 us
  transfers between devices with their start and end apart: 7 -> 7, of which waited for: 1 -> 1; matrix products, arithmetic and copies ran while one was open for 13% -> 4% of each run, Pallas kernels for 0% -> 0%
where the time goes in v1:
time: 1220 us
  waiting for transfers between devices  1070 us (88%)
  other arithmetic  47.1 us (4%)
  local copies, waits for them, and re-layouts  46.5 us (4%)
  matrix products  20.4 us (2%)
  between operations  16 us (1%)
  starting transfers between devices  12.7 us (1%)
    all_gather x1, waiting for transfers between devices, body(): total = jnp.sum(lax.all_gather(local_grad, 'space'), axis=0)  1070 us
    unnamed x105, local copies, waits for them, and re-layouts  35.3 us
  transfers between devices with their start and end apart: 7, of which 1 were waited for; matrix products, arithmetic and copies ran while one was open for 4% of the time, Pallas kernels for 0%

profile of v1, /device:TPU:0, one launch (start us, length us, event | category | flops | bytes accessed | tf_op | source)
XLA Modules:
  0.0 1220.9 jit_solution(5308959309423740087)
XLA Ops:
  8.0 7.4 all_gather.9
  15.4 1.3 collective-permute-start.1
  16.7 5.3 collective-permute-start
  22.0 2.3 all_gather.10
  24.3 1.3 collective-permute-start.3
  25.5 4.6 collective-permute-start.2
  30.1 3.1 fusion.87
  33.2 0.9 copy.71
  34.1 0.9 copy.70
  35.0 0.9 copy.69
  36.0 0.9 copy.68
  36.9 0.9 copy.67
  37.8 0.9 copy.66
  38.8 0.9 copy.65
  39.7 1.9 copy.64
  41.6 1.9 copy.63
  43.6 1.5 select_maximum_fusion
  45.7 1.5 select_maximum_fusion.2
  47.2 2.0 slice_multiply_fusion.24
  49.3 3.0 slice_multiply_fusion.2
  52.7 1.1 broadcast_multiply_fusion.3
  55.5 2.7 slice_multiply_fusion.26
  59.9 1.2 fusion.11
  62.5 1.2 pad_maximum_fusion
  66.1 1.0 pad_maximum_fusion.2
  69.5 1.3 pad_maximum_fusion.4
  72.0 1.3 pad_maximum_fusion.6
  73.4 0.9 copy-done.39
  76.4 1.2 fusion.10
  77.6 1.3 fusion.9
  79.0 1.3 fusion.8
  80.2 1.3 fusion.7
  81.5 1.3 fusion.6
  82.8 1.3 fusion.5
  84.1 1.3 fusion.4
  85.4 1.3 fusion.3
  86.7 1.3 fusion.2
  87.9 1.3 fusion.1
  89.2 8.1 copy.57
  97.4 1.0 convert_element_type.136
  98.4 0.8 copy.60
  99.1 1.0 convert_element_type.135
  100.1 0.8 copy.59
  100.9 1068.4 %all-gather.2.cloned.1.call-done = f32[8,3,3,3,256,256]{5,4,3,2,1,0:T(8,128)} async-done(((f32[1,3,3,3,256,256]{5,4,3,2,1,0:T(8,128)}), f32[8,3,3,3,256,256]{5,4,3,2,1,0:T(8,128)}) %all-gather.2.cloned.1.call-update) | async-done | bytes 56623120 | tf_op jit(solution)/shard_map/all_gather | solution.py:74
  1169.3 21.5 %reduce_sum.9 = f32[3,3,3,256,256]{4,3,2,1,0:T(8,128)} reduce(f32[8,3,3,3,256,256]{5,4,3,2,1,0:T(8,128)} %all-gather.2.cloned.1.call-done, f32[]{:T(128)} %constant.33.clone.1), dimensions={0}, to_apply=%region_2.3 | reduce | flops 12386304 | bytes 63700996 | tf_op jit(solution)/shard_map/reduce_sum | solution.py:74
  1190.7 8.1 copy.62
  1198.8 6.5 broadcast_multiply_fusion
  1205.4 8.0 copy.61
  (124 shorter events, 13.9 us)
Async XLA Ops:
  8.0 89.4 %reduce-scatter.5.cloned.1.call-start = ((), (), s32[]{:S(2)}) async-start(), calls=%async_computation.3 | async-start | bytes 786432 | tf_op jit(solution)/shard_map/reduce_scatter | solution.py:70
  15.4 30.3 %collective-permute-start.1 = (bf16[1,256,512]{2,1,0:T(8,128)(2,1)S(1)}, bf16[1,256,512]{2,1,0:T(8,128)(2,1)}, u32[]{:S(2)}, u32[]{:S(2)}) collective-permute-start(bf16[1,256,512]{2,1,0:T(8,128)(2,1)S(1)} %all_gather.9), channel_id=1, source_target_pairs={{4,0},{8,4},{12,8},{16,12},{20,16},{24,20},{28,24},{5,1},{9,5},{13... | collective-permute-start | bytes 786440 | tf_op jit(solution)/shard_map/ppermute | solution.py:17
  16.7 29.0 %collective-permute-start = (bf16[1,256,512]{2,1,0:T(8,128)(2,1)S(1)}, bf16[1,256,512]{2,1,0:T(8,128)(2,1)}, u32[]{:S(2)}, u32[]{:S(2)}) collective-permute-start(bf16[1,256,512]{2,1,0:T(8,128)(2,1)S(1)} %all_gather.9), channel_id=1, source_target_pairs={{0,4},{4,8},{8,12},{12,16},{16,20},{20,24},{24,28},{1,5},{5,9},{9,... | collective-permute-start | bytes 786440 | tf_op jit(solution)/shard_map/ppermute | solution.py:16
  24.3 19.3 %collective-permute-start.3 = (bf16[1,256,512]{2,1,0:T(8,128)(2,1)S(1)}, bf16[1,256,512]{2,1,0:T(8,128)(2,1)}, u32[]{:S(2)}, u32[]{:S(2)}) collective-permute-start(bf16[1,256,512]{2,1,0:T(8,128)(2,1)S(1)} %all_gather.10), channel_id=1, source_target_pairs={{4,0},{8,4},{12,8},{16,12},{20,16},{24,20},{28,24},{5,1},{9,5},{13... | collective-permute-start | bytes 786440 | tf_op jit(solution)/shard_map/ppermute | solution.py:17
  25.5 18.0 %collective-permute-start.2 = (bf16[1,256,512]{2,1,0:T(8,128)(2,1)S(1)}, bf16[1,256,512]{2,1,0:T(8,128)(2,1)S(1)}, u32[]{:S(2)}, u32[]{:S(2)}) collective-permute-start(bf16[1,256,512]{2,1,0:T(8,128)(2,1)S(1)} %all_gather.10), channel_id=1, source_target_pairs={{0,4},{4,8},{8,12},{12,16},{16,20},{20,24},{24,28},{1,5},{5,9},{9,... | collective-permute-start | bytes 786440 | tf_op jit(solution)/shard_map/ppermute | solution.py:16
  43.6 2.1 copy-start.18
  49.3 12.1 copy-start.17
  49.3 3.0 copy-start.6
  52.3 1.5 copy-start.5
  53.7 17.5 %copy-start.12 = (bf16[1,256,512]{2,1,0:T(8,128)(2,1)}, bf16[1,256,512]{2,1,0:T(8,128)(2,1)S(1)}, u32[]{:S(2)}) copy-start(bf16[1,256,512]{2,1,0:T(8,128)(2,1)S(1)} %get-tuple-element.89) | copy-start | bytes 786436
  54.6 1.0 copy-start.19
  58.2 3.2 copy-start.32
  59.9 1.5 copy-start.33
  59.9 1.5 copy-start.45
  61.1 38.0 %reduce-scatter.3.cloned.1.call-start = ((), (), s32[]{:S(2)}) async-start(), calls=%async_computation.2 | async-start | bytes 786432 | tf_op jit(solution)/shard_map/reduce_scatter | solution.py:69
  61.4 1.0 copy-start.21
  61.4 1.1 copy-start.31
  62.5 1.2 copy-start.44
  63.8 1.0 copy-start.29
  63.8 1.1 copy-start.30
  63.8 1.2 copy-start.43
  65.0 1.0 copy-start.27
  65.0 1.1 copy-start.28
  66.1 1.0 copy-start.42
  67.1 1.0 copy-start.15
  67.1 1.1 copy-start.26
  67.1 1.2 copy-start.41
  68.4 1.0 copy-start.9
  68.4 1.0 copy-start.24
  68.4 1.1 copy-start.25
  69.5 1.3 copy-start.40
  70.8 1.0 copy-start.8
  70.8 1.1 copy-start.20
  70.8 1.2 copy-start.22
  70.8 1.2 copy-start.23
  72.0 1.3 copy-start.34
  72.0 1.3 copy-start.35
  72.0 1.3 copy-start.36
  73.3 1.0 copy-start.39
  74.3 1.0 copy-start.13
  74.3 1.1 copy-start.38
  75.4 1.0 copy-start.37
  78.9 1.4 copy-start
  78.9 1090.4 %all-gather.2.cloned.1.call-start = ((), (), s32[]{:S(2)}) async-start(), calls=%async_computation.4 | async-start | bytes 63700992 | tf_op jit(solution)/shard_map/all_gather | solution.py:74
  80.2 2.6 copy-start.2
  81.5 2.6 copy-start.1
  82.8 2.6 copy-start.4
  84.1 2.6 copy-start.3
  (5 other events, 4.8 us)
Sparse Core Ops, SparseCore 0:
  61.3 16.0 reduce-scatter.4
  79.7 8.7 reduce-scatter.2
Sparse Core Ops, SparseCore 1:
  97.4 1071.8 all-gather.1
